TPU v7x, 256 devices: a whole 4x4x8 slice. The times are simulated.
256 devices in a mesh: pts: 8 (over x, core), rows: 32 (over z, y).
Axes of the slice: x: 4, y: 4, z: 8, core: 2. Of those that a mesh axis runs over, the one named last changes fastest.
Arguments:
- solutions: bfloat16 [16, 262144, 128], P('pts', 'rows'), may hold values from -6 to 6
- probe: bfloat16 [64, 262144], P(None, 'rows'), may hold values from -0.01171875 to 0.01171875
- left_factor: float32 [256, 256], replicated, may hold values from -0.375 to 0.375
- singular: float32 [256], replicated, may hold values from 1 to 13.8, as said below
- right_factor: float32 [256, 256], replicated, may hold values from -0.375 to 0.375
- reduced_adjoint: float32 [256, 256], replicated, may hold values from -6 to 6
Outputs:
- solution_adjoint: bfloat16 [16, 262144, 128], P('pts', 'rows')
Inputs may be any that keep to these rules, and one draw needn't show every extreme that they name: `singular`: rising, each value at least 0.03 above the one before.
All inputs are finite; a program needn't handle non-finite values.
Results may differ from a plain program's by a relative error of at most 0.0049.
Values sent between devices are 32-bit elements; how exact they have to be, the bound alone decides.
A program may use at most 64 MiB of HBM per device.

v0:
```python
import math
import jax
import jax.numpy as jnp
from jax import lax
from jax.sharding import PartitionSpec as P

L = 64
K = 4


def coefficients(first, count, total, orders):
    theta = math.pi * (first + jnp.arange(count, dtype=jnp.float32) + 0.5) / total
    angle = theta[:, None] * orders[None, :]
    return (jnp.cos(angle) / total, jnp.sin(angle) / total)


def matmul(first, second):
    return jnp.dot(
        first, second, precision=lax.Precision.HIGHEST, preferred_element_type=jnp.float32
    )


def svd_back(hankel, left, sing, right, adjoint):
    quot = matmul(left.T, hankel)
    prod_right = matmul(hankel, right)
    zmat = matmul(quot, right)
    zbar = adjoint / sing[None, :]
    sbar = -jnp.sum(adjoint * zmat, axis=0) / (sing * sing)
    ubar = matmul(prod_right, zbar.T)
    wbar = matmul(quot.T, zbar)
    left_term = matmul(left.T, ubar)
    right_term = matmul(right.T, wbar)
    square = sing * sing
    eye_mask = jnp.eye(sing.shape[0], dtype=bool)
    recip = jnp.where(
        eye_mask, 0.0, 1.0 / jnp.where(eye_mask, 1.0, square[None, :] - square[:, None])
    )
    core = (
        recip * (left_term - left_term.T) * sing[None, :]
        + jnp.diag(sbar)
        + sing[:, None] * (recip * (right_term - right_term.T))
    )
    return (core, zbar)


def build_hankel(moments):
    return jnp.concatenate(
        [jnp.concatenate([moments[i + j] for j in range(K)], axis=1) for i in range(K)], axis=0
    )


def per_device(solutions, probe, left_factor, singular, right_factor, reduced_adjoint):
    hi = lax.Precision.HIGHEST
    point_count = solutions.shape[0]
    total = point_count * lax.axis_size("pts")
    first = (lax.axis_index("pts") * point_count).astype(jnp.float32)
    orders = jnp.arange(1, 2 * K + 1, dtype=jnp.float32)
    cos_t, sin_t = coefficients(first, point_count, total, orders)
    gram = jnp.einsum("ln,pnc->plc", probe, solutions, preferred_element_type=jnp.float32)
    moments = lax.psum(
        jnp.einsum("pk,plc->klc", cos_t[:, 1:], gram[:, :, :L], precision=hi)
        - jnp.einsum("pk,plc->klc", sin_t[:, 1:], gram[:, :, L:], precision=hi),
        ("pts", "rows"),
    )
    hankel = build_hankel(moments)
    core, zbar = svd_back(hankel, left_factor, singular, right_factor, reduced_adjoint)
    first_bar = matmul(matmul(left_factor, core), right_factor.T)
    second_bar = matmul(matmul(left_factor, zbar), right_factor.T)
    blocks = [jnp.zeros((L, L), jnp.float32) for k in range(2 * K)]
    for i in range(K):
        for j in range(K):
            blocks[i + j] = blocks[i + j] + first_bar[i * L : (i + 1) * L, j * L : (j + 1) * L]
            blocks[i + j + 1] = (
                blocks[i + j + 1] + second_bar[i * L : (i + 1) * L, j * L : (j + 1) * L]
            )
    moment_adjoint = jnp.stack(blocks)
    weights = jnp.concatenate(
        [
            jnp.einsum("pk,klc->plc", cos_t, moment_adjoint, precision=hi),
            -jnp.einsum("pk,klc->plc", sin_t, moment_adjoint, precision=hi),
        ],
        axis=2,
    ).astype(jnp.bfloat16)
    result = jnp.einsum("ln,plc->pnc", probe, weights, preferred_element_type=jnp.float32)
    return result.astype(jnp.bfloat16)


def solution(mesh):
    in_specs = (P("pts", "rows", None), P(None, "rows"), P(), P(), P(), P())
    out_specs = P("pts", "rows", None)
    return jax.shard_map(
        per_device, mesh=mesh, in_specs=in_specs, out_specs=out_specs, check_vma=False
    )
```

profile of v0, /device:TPU:2, one launch (start us, length us, event | category | flops | bytes accessed | tf_op | source)
XLA Modules:
  0.0 296.1 jit_solution(6354948563807823471)
XLA Ops:
  6.6 1.1 copy-done
  7.8 3.0 %convolution_bitcast_fusion = f32[2,64,128]{2,1,0:T(8,128)S(1)} fusion(bf16[2,8192,128]{2,1,0:T(8,128)(2,1)} %param.6, bf16[64,8192]{1,0:T(8,128)(2,1)S(1)} %copy-done), kind=kOutput, calls=%fused_computation.5 | convolution fusion | flops 268435456 | bytes 5308416 | tf_op jit(solution)/shard_map/ln,pnc->plc/dot_general | solution.py:59
  10.7 0.1 fusion.69
  10.8 0.1 fusion.51
  10.9 0.5 fusion.31
  11.5 1.2 convolution_subtract_fusion
  12.7 0.6 fusion.63
  13.3 0.6 fusion.73
  13.9 256.3 %all-reduce.2.cloned.1.call-done = f32[7,64,64]{2,0,1:T(8,128)} async-done(((f32[7,64,64]{2,0,1:T(8,128)}), f32[7,64,64]{2,0,1:T(8,128)}) %all-reduce.2.cloned.1.call-update) | async-done | bytes 114704 | tf_op jit(solution)/shard_map/psum | solution.py:60
  270.3 2.1 fusion.68
  272.4 0.7 fusion.66
  273.1 0.6 fusion.1
  273.7 0.4 fusion.64
  274.1 0.4 fusion.67
  274.6 0.6 fusion.71
  275.2 0.4 fusion.65
  275.6 0.6 fusion.70
  276.2 0.1 copy.15
  276.4 0.1 copy.16
  276.5 0.7 fusion.7
  277.3 0.6 fusion.72
  277.9 0.1 fusion.45
  277.9 0.1 fusion.43
  278.0 0.1 fusion.41
  278.1 0.1 fusion.39
  278.2 0.1 fusion.37
  278.3 0.1 fusion.35
  278.4 0.1 fusion.33
  278.5 0.5 fusion.20
  279.0 0.5 fusion.18
  279.6 3.3 %fusion = bf16[2,8192,128]{1,2,0:T(8,128)(2,1)} fusion(bf16[64,8192]{1,0:T(8,128)(2,1)S(1)} %copy-done, bf16[2,64,64]{2,1,0:T(8,128)(2,1)S(1)} %fusion.29, bf16[2,64,64]{2,1,0:T(8,128)(2,1)S(1)} %copy.39), kind=kOutput, calls=%fused_computation.1 | convolution fusion | flops 270598144 | bytes 5275648 | tf_op jit(solution)/shard_map/ln,plc->pnc/dot_general | solution.py:84
  282.9 6.3 %copy.17 = bf16[2,8192,128]{2,1,0:T(8,128)(2,1)} copy(bf16[2,8192,128]{1,2,0:T(8,128)(2,1)} %fusion) | data formatting | bytes 8388608 | tf_op jit(solution)/shard_map/convert_element_type | solution.py:85
  (17 shorter events, 0.1 us)
Async XLA Ops:
  6.5 1.2 copy-start
  6.5 6.2 %copy-start.4 = (f32[256]{0:T(256)S(1)}, f32[256]{0:T(256)}, u32[]{:S(2)}) copy-start(f32[256]{0:T(256)} %param.9) | copy-start | bytes 3076
  6.5 6.2 %copy-start.3 = (f32[256,256]{1,0:T(8,128)S(1)}, f32[256,256]{1,0:T(8,128)}, u32[]{:S(2)}) copy-start(f32[256,256]{1,0:T(8,128)} %param.11) | copy-start | bytes 786436
  6.5 6.2 %copy-start.2 = (f32[256,256]{1,0:T(8,128)S(1)}, f32[256,256]{1,0:T(8,128)}, u32[]{:S(2)}) copy-start(f32[256,256]{1,0:T(8,128)} %param.8) | copy-start | bytes 786436
  6.5 6.8 %copy-start.1 = (f32[256,256]{1,0:T(8,128)S(1)}, f32[256,256]{1,0:T(8,128)}, u32[]{:S(2)}) copy-start(f32[256,256]{1,0:T(8,128)} %param.10) | copy-start | bytes 786436
  6.5 263.7 %all-reduce.2.cloned.1.call-start = ((), (), s32[]{:S(2)}) async-start(), calls=%async_computation | async-start | bytes 524288 | tf_op jit(solution)/shard_map/psum | solution.py:60
Sparse Core Ops, SparseCore 0:
  12.8 257.4 all-reduce.1
where the time goes:
time: 296 us
  waiting for transfers between devices  256 us (86%)
  matrix products  15.4 us (5%)
  between operations  13.7 us (5%)
  local copies, waits for them, and re-layouts  9.97 us (3%)
    psum x1, waiting for transfers between devices, per_device(): lax.psum(jnp.einsum('pk,plc->klc', cos_t[:, 1:], gram[:, :, :L], precisio...  256 us
    dot_general x11, matrix products, matmul(): jnp.dot(first, second, precision=lax.Precision.HIGHEST, preferred_element...  6.33 us
    convert_element_type x1, local copies, waits for them, and re-layouts, per_device(): return result.astype(jnp.bfloat16)  6.31 us
  transfers between devices with their start and end apart: 1, of which 1 were waited for; matrix products, arithmetic and copies ran while one was open for 0% of the time, Pallas kernels for 0%

commit v1 on v0

--- a/solution.py
+++ b/solution.py
@@ -6,6 +6,11 @@
 
 L = 64
 K = 4
+
+
+def axis_by_axis(array, leading, second_2):
+    partial = lax.psum(array, leading)
+    return lax.psum(partial, second_2)
 
 
 def coefficients(first, count, total, orders):
@@ -57,10 +62,11 @@
     orders = jnp.arange(1, 2 * K + 1, dtype=jnp.float32)
     cos_t, sin_t = coefficients(first, point_count, total, orders)
     gram = jnp.einsum("ln,pnc->plc", probe, solutions, preferred_element_type=jnp.float32)
-    moments = lax.psum(
+    moments = axis_by_axis(
         jnp.einsum("pk,plc->klc", cos_t[:, 1:], gram[:, :, :L], precision=hi)
         - jnp.einsum("pk,plc->klc", sin_t[:, 1:], gram[:, :, L:], precision=hi),
-        ("pts", "rows"),
+        "pts",
+        "rows",
     )
     hankel = build_hankel(moments)
     core, zbar = svd_back(hankel, left_factor, singular, right_factor, reduced_adjoint)

time: 296 us -> 256 us (0.86)
  waiting for transfers between devices: 256 us -> 216 us
    psum x1 -> x2, waiting for transfers between devices: 256 us -> 216 us  [the longest x1 150 us: axis_by_axis(): return lax.psum(partial, second_2)]
  transfers between devices with their start and end apart: 1 -> 2, of which waited for: 1 -> 2; matrix products, arithmetic and copies ran while one was open for 0% -> 0% of each run, Pallas kernels for 0% -> 0%
where the time goes in v1:
time: 256 us; the launch traced here: 255 us
  waiting for transfers between devices  216 us (84%)
  matrix products  15.4 us (6%)
  between operations  13.7 us (5%)
  local copies, waits for them, and re-layouts  10.1 us (4%)
    psum x1, waiting for transfers between devices, axis_by_axis(): return lax.psum(partial, second_2)  150 us
    psum x1, waiting for transfers between devices, axis_by_axis(): partial = lax.psum(array, leading)  65.6 us
    dot_general x11, matrix products, matmul(): jnp.dot(first, second, precision=lax.Precision.HIGHEST, preferred_element...  6.32 us
    convert_element_type x1, local copies, waits for them, and re-layouts, per_device(): return result.astype(jnp.bfloat16)  6.31 us
  transfers between devices with their start and end apart: 2, of which 2 were waited for; matrix products, arithmetic and copies ran while one was open for 0% of the time, Pallas kernels for 0%

profile of v1, /device:TPU:2, one launch (start us, length us, event | category | flops | bytes accessed | tf_op | source)
XLA Modules:
  0.0 255.4 jit_solution(12980207501158944608)
XLA Ops:
  6.6 1.1 copy-done
  7.8 3.0 %convolution_bitcast_fusion = f32[2,64,128]{2,1,0:T(8,128)S(1)} fusion(bf16[2,8192,128]{2,1,0:T(8,128)(2,1)} %param.6, bf16[64,8192]{1,0:T(8,128)(2,1)S(1)} %copy-done), kind=kOutput, calls=%fused_computation.5 | convolution fusion | flops 268435456 | bytes 5308416 | tf_op jit(solution)/shard_map/ln,pnc->plc/dot_general | solution.py:64
  10.7 0.1 fusion.69
  10.8 0.1 fusion.51
  10.9 0.5 fusion.31
  11.5 1.2 convolution_subtract_fusion
  12.8 0.6 fusion.63
  13.4 65.6 %all-reduce.3.cloned.1.call-done = f32[7,64,64]{2,0,1:T(8,128)} async-done(((f32[7,64,64]{2,0,1:T(8,128)}), f32[7,64,64]{2,0,1:T(8,128)}) %all-reduce.3.cloned.1.call-update) | async-done | bytes 114704 | tf_op jit(solution)/shard_map/psum | solution.py:12
  79.0 0.6 fusion.73
  79.6 149.9 %all-reduce.5.cloned.1.call-done = f32[7,64,64]{2,0,1:T(8,128)} async-done(((f32[7,64,64]{2,0,1:T(8,128)}), f32[7,64,64]{2,0,1:T(8,128)}) %all-reduce.5.cloned.1.call-update) | async-done | bytes 114704 | tf_op jit(solution)/shard_map/psum | solution.py:13
  229.5 2.2 fusion.68
  231.7 0.7 fusion.66
  232.4 0.6 fusion.1
  233.0 0.4 fusion.64
  233.4 0.4 fusion.67
  233.9 0.6 fusion.71
  234.5 0.4 fusion.65
  234.9 0.6 fusion.70
  235.5 0.1 copy.15
  235.7 0.1 copy.16
  235.8 0.7 fusion.7
  236.6 0.6 fusion.72
  237.2 0.1 fusion.45
  237.3 0.1 fusion.43
  237.4 0.1 fusion.41
  237.5 0.1 fusion.39
  237.6 0.1 fusion.37
  237.7 0.1 fusion.35
  237.8 0.5 fusion.20
  238.4 0.5 fusion.18
  238.9 3.3 %fusion = bf16[2,8192,128]{1,2,0:T(8,128)(2,1)} fusion(bf16[64,8192]{1,0:T(8,128)(2,1)S(1)} %copy-done, bf16[2,64,64]{2,1,0:T(8,128)(2,1)S(1)} %fusion.29, bf16[2,64,64]{2,1,0:T(8,128)(2,1)S(1)} %copy.39), kind=kOutput, calls=%fused_computation.1 | convolution fusion | flops 270598144 | bytes 5275648 | tf_op jit(solution)/shard_map/ln,plc->pnc/dot_general | solution.py:90
  242.2 6.3 %copy.17 = bf16[2,8192,128]{2,1,0:T(8,128)(2,1)} copy(bf16[2,8192,128]{1,2,0:T(8,128)(2,1)} %fusion) | data formatting | bytes 8388608 | tf_op jit(solution)/shard_map/convert_element_type | solution.py:91
  (20 shorter events, 0.2 us)
Async XLA Ops:
  6.5 1.2 copy-start
  6.5 6.2 %copy-start.4 = (f32[256]{0:T(256)S(1)}, f32[256]{0:T(256)}, u32[]{:S(2)}) copy-start(f32[256]{0:T(256)} %param.9) | copy-start | bytes 3076
  6.5 6.2 %copy-start.3 = (f32[256,256]{1,0:T(8,128)S(1)}, f32[256,256]{1,0:T(8,128)}, u32[]{:S(2)}) copy-start(f32[256,256]{1,0:T(8,128)} %param.11) | copy-start | bytes 786436
  6.5 6.2 %copy-start.2 = (f32[256,256]{1,0:T(8,128)S(1)}, f32[256,256]{1,0:T(8,128)}, u32[]{:S(2)}) copy-start(f32[256,256]{1,0:T(8,128)} %param.8) | copy-start | bytes 786436
  6.5 72.4 %copy-start.1 = (f32[256,256]{1,0:T(8,128)S(1)}, f32[256,256]{1,0:T(8,128)}, u32[]{:S(2)}) copy-start(f32[256,256]{1,0:T(8,128)} %param.10) | copy-start | bytes 786436
  6.5 72.4 %all-reduce.3.cloned.1.call-start = ((), (), s32[]{:S(2)}) async-start(), calls=%async_computation | async-start | bytes 524288 | tf_op jit(solution)/shard_map/psum | solution.py:12
  12.7 216.8 %all-reduce.5.cloned.1.call-start = ((), (), s32[]{:S(2)}) async-start(), calls=%async_computation.1 | async-start | bytes 524288 | tf_op jit(solution)/shard_map/psum | solution.py:13
Sparse Core Ops, SparseCore 0:
  12.8 66.1 all-reduce.2
  82.4 147.0 all-reduce.4
